TPU v7x, 128 devices: a whole 4x4x4 slice. The times are simulated.
128 devices in a mesh: tm: 8 (over y_lo, x), chan: 16 (over z, y_hi, core).
Axes of the slice: x: 4, y: 4 (y_hi: 2, y_lo: 2; y = y_hi * 2 + y_lo), z: 4, core: 2. Of those that a mesh axis runs over, the one named last changes fastest.
Arguments:
- samples: bfloat16 [1024, 262144], P('tm', 'chan'), may hold values from -6 to 6
- valid: int32 [1024, 32], P('tm', 'chan'), may hold values from 0 to 1, as said below
Outputs:
- average: float32 [1024, 4224], P(('tm', 'chan'))
Inputs may be any that keep to these rules, and one draw needn't show every extreme that they name: `valid`: split the channels into aligned groups of 128; in every segment each group has at most 96 entries equal to 1, and exactly 96 for some group and segment; at least one channel has no 1 in any segment.
All inputs are finite; a program needn't handle non-finite values.
Results may differ from a plain program's by a relative error of at most 0.0026.
Values may be sent and summed in bfloat16 or wider, within the bound.
A program may use at most 128 MiB of HBM per device.

v0:
```python
import jax
import jax.numpy as jnp
from jax import lax
from jax.sharding import PartitionSpec as P

RADIX = 128
KBANDS = 33
full_turn = 6.283185307179586


def make_tables():
    seg_len = RADIX * RADIX
    counter = jnp.arange(RADIX, dtype=jnp.int32)
    inner_prod = counter[:, None] * counter[None, :] % RADIX
    angle_one = full_turn * inner_prod.astype(jnp.float32) / RADIX
    cos_one = jnp.cos(angle_one).astype(jnp.bfloat16)
    sin_one = jnp.sin(angle_one).astype(jnp.bfloat16)
    outer_prod = counter[:, None] * counter[None, :] % seg_len
    angle_mid = full_turn * outer_prod.astype(jnp.float32) / seg_len
    twid_real = jnp.cos(angle_mid)
    twid_imag = -jnp.sin(angle_mid)
    band_index = jnp.arange(KBANDS, dtype=jnp.int32)
    angle_two = (
        full_turn * (counter[:, None] * band_index[None, :] % RADIX).astype(jnp.float32) / RADIX
    )
    cos_two = jnp.cos(angle_two).astype(jnp.bfloat16)
    sine_double_angle = jnp.sin(angle_two).astype(jnp.bfloat16)
    places = jnp.arange(seg_len, dtype=jnp.int32).astype(jnp.float32)
    window = 0.5 - 0.5 * jnp.cos(full_turn * places / seg_len)
    weight_sum = jnp.sum(window * window)
    onesided = (
        jnp.where(jnp.arange(KBANDS * RADIX, dtype=jnp.int32) == 0, 1.0, 2.0).astype(jnp.float32)
        / weight_sum
    )
    return (cos_one, sin_one, twid_real, twid_imag, cos_two, sine_double_angle, window, onesided)


def contract(left, right, form):
    return jnp.einsum(form, left, right, preferred_element_type=jnp.float32)


def spectrum(segment, tables):
    cos_one, sin_one, twid_real, twid_imag, cos_two, sine_double_angle, window, onesided = tables
    height = segment.shape[0]
    values = segment.astype(jnp.float32)
    centred = values - jnp.mean(values, axis=1, keepdims=True)
    shaped = (centred * window[None, :]).astype(jnp.bfloat16).reshape(height, RADIX, RADIX)
    first_real = contract(shaped, cos_one, "cnm,nk->ckm")
    first_imag = -contract(shaped, sin_one, "cnm,nk->ckm")
    mid_real = (first_real * twid_real - first_imag * twid_imag).astype(jnp.bfloat16)
    mid_imag = (first_real * twid_imag + first_imag * twid_real).astype(jnp.bfloat16)
    last_real = contract(mid_real, cos_two, "ckn,nm->cmk") + contract(
        mid_imag, sine_double_angle, "ckn,nm->cmk"
    )
    closing_quadrature_part = contract(mid_imag, cos_two, "ckn,nm->cmk") - contract(
        mid_real, sine_double_angle, "ckn,nm->cmk"
    )
    return (last_real * last_real + closing_quadrature_part * closing_quadrature_part).reshape(
        height, -1
    ) * onesided[None, :]


def block_power(leading, trailing, tables):
    height = leading.shape[0]
    block_rows = 128
    segments = jnp.concatenate([leading, trailing], axis=1)

    def one_block(piece):
        return spectrum(piece, tables)

    final_output = lax.map(one_block, segments.reshape(height // block_rows, block_rows, -1))
    return final_output.reshape(height, -1)


def per_device(samples, valid):
    tables = make_tables()
    half_len = RADIX * RADIX // 2
    moved_samples, moved_valid = (
        lax.all_to_all(samples, "chan", split_axis=0, concat_axis=1, tiled=True),
        lax.all_to_all(valid.astype(jnp.bfloat16), "chan", split_axis=0, concat_axis=1, tiled=True),
    )
    owned_rows = moved_samples.shape[0]
    record = jnp.concatenate(
        [moved_samples, jnp.zeros((owned_rows, half_len), jnp.bfloat16)], axis=1
    )
    blocks = record.reshape(owned_rows, -1, half_len)
    leading = blocks[:, :-1].reshape(-1, half_len)
    trailing = blocks[:, 1:].reshape(-1, half_len)
    powers = block_power(leading, trailing, tables).reshape(owned_rows, blocks.shape[1] - 1, -1)
    weights = moved_valid.astype(jnp.float32)
    totals = jnp.sum(weights[:, :, None] * powers, axis=1)
    tallied_count = jnp.sum(weights, axis=1)
    return totals / jnp.maximum(tallied_count, 1.0)[:, None]


def solution(mesh):
    return jax.shard_map(
        per_device,
        mesh=mesh,
        in_specs=(P("tm", "chan"), P("tm", "chan")),
        out_specs=P(("tm", "chan"), None),
        check_vma=False,
    )
```

profile of v0, /device:TPU:1, one launch (start us, length us, event | category | flops | bytes accessed | tf_op | source)
XLA Modules:
  0.0 189.5 jit_solution(12834739281329465822)
XLA Ops:
  0.8 16.3 %all_to_all.32 = bf16[16,8,2]{1,2,0:T(2,128)(2,1)S(1)} all-to-all(bf16[16,8,2]{1,2,0:T(2,128)(2,1)S(1)} %copy.36), channel_id=1, replica_groups=mesh['tm'=8,'chan'=16] {'chan'}, dimensions={0} | all-to-all | bytes 1024 | tf_op jit(solution)/shard_map/all_to_all | solution.py:80
  17.1 4.9 %all-to-all-start.1 = ((bf16[16,8,16384]{2,1,0:T(8,128)(2,1)}), bf16[16,8,16384]{2,1,0:T(8,128)(2,1)}, u32[]{:S(2)}, u32[]{:S(2)}) async-start(bf16[16,8,16384]{2,1,0:T(8,128)(2,1)} %bitcast.100), calls=%async_computation.1 | async-start | bytes 8388608 | tf_op jit(solution)/shard_map/all_to_all | solution.py:79
  24.0 49.0 %all-to-all-done.1 = bf16[16,8,16384]{2,1,0:T(8,128)(2,1)} async-done(((bf16[16,8,16384]{2,1,0:T(8,128)(2,1)}), bf16[16,8,16384]{2,1,0:T(8,128)(2,1)}, u32[]{:S(2)}, u32[]{:S(2)}) %all-to-all-start.1) | async-done | bytes 4194336 | tf_op jit(solution)/shard_map/all_to_all | solution.py:79
  73.0 3.0 %concatenate.11 = bf16[8,270336]{1,0:T(8,128)(2,1)S(1)} pad(bf16[8,262144]{1,0:T(8,128)(2,1)} %bitcast.4, bf16[]{:T(256)} %constant.69.clone.1), padding=0_0x0_8192 | pad | bytes 8519682 | tf_op jit(solution)/shard_map/concatenate | solution.py:83
  76.0 0.9 fusion.80
  77.0 4.3 %copy.38 = bf16[8,32,8192]{2,1,0:T(8,128)(2,1)} copy(bf16[8,32,8192]{2,0,1:T(8,128)(2,1)S(1)} %get-tuple-element.140) | data formatting | bytes 8388608 | tf_op jit(solution)/shard_map/slice | solution.py:87
  81.2 4.3 %copy.39 = bf16[8,32,8192]{2,1,0:T(8,128)(2,1)} copy(bf16[8,32,8192]{2,0,1:T(8,128)(2,1)S(1)} %get-tuple-element.141) | data formatting | bytes 8388608 | tf_op jit(solution)/shard_map/slice | solution.py:88
  85.5 7.6 %pad_maximum_fusion = bf16[2,128,16384]{2,1,0:T(8,128)(2,1)} fusion(bf16[2,128,8192]{2,1,0:T(8,128)(2,1)} %bitcast.98, bf16[2,128,8192]{2,1,0:T(8,128)(2,1)} %bitcast.97), kind=kLoop, calls=%fused_computation.92 | loop fusion | flops 16777216 | bytes 16777216 | tf_op jit(solution)/shard_map/concatenate | solution.py:66
  93.1 92.8 %while.12 = (s32[]{:T(128)}, f32[2,128,4224]{2,1,0:T(8,128)}, bf16[2,128,16384]{2,1,0:T(8,128)(2,1)}, f32[]{:T(128)}, s32[]{:T(128)}) while((s32[]{:T(128)}, f32[2,128,4224]{2,1,0:T(8,128)}, bf16[2,128,16384]{2,1,0:T(8,128)(2,1)}, f32[]{:T(128)}, s32[]{:T(128)}) %tuple.31), condition=%wide.region_3.4_spmd.clone.clone, body=%wide.region_1.3_spmd.clone.clone.sunk | while | flops 1669451648 | bytes 142118992 | solution.py:71
  93.1 3.0 %convert_bitcast_fusion.2 = f32[16,8,128,128]{3,1,2,0:T(8,128)S(1)} fusion(bf16[2,128,16384]{2,1,0:T(8,128)(2,1)} %get-tuple-element.187, s32[]{:T(128)} %get-tuple-element.180), kind=kLoop, calls=%fused_computation.9.clone.1 | loop fusion | flops 2097152 | bytes 12582916 | tf_op jit(solution)/shard_map/while
  96.1 4.7 %copy.56 = f32[16,8,128,128]{3,2,1,0:T(8,128)} copy(f32[16,8,128,128]{3,1,2,0:T(8,128)S(1)} %convert_bitcast_fusion.2) | data formatting | bytes 16777216 | tf_op jit(solution)/shard_map/while
  100.8 9.0 %copy.57 = f32[128,128,128]{1,2,0:T(8,128)} copy(f32[128,128,128]{2,1,0:T(8,128)} %bitcast.95) | data formatting | bytes 16777216 | tf_op jit(solution)/shard_map/while/body/eval_jaxpr/convert_element_type | solution.py:45
  109.8 2.8 %convert_reduce_fusion.3 = f32[128]{0:T(128)S(1)} fusion(bf16[2,128,16384]{2,1,0:T(8,128)(2,1)} %get-tuple-element.187, s32[]{:T(128)} %get-tuple-element.180), kind=kLoop, calls=%fused_computation.8.clone.1 | loop fusion | flops 4194176 | bytes 4194820 | tf_op jit(solution)/shard_map/while/body/eval_jaxpr/reduce_sum | solution.py:46
  112.9 4.9 %fusion.108 = f32[128,128,128]{2,1,0:T(8,128)S(1)} fusion(f32[128,128,128]{1,2,0:T(8,128)} %copy.57, f32[128,128]{0,1:T(8,128)S(1)} %copy.58, f32[128]{0:T(128)S(1)} %broadcast_multiply_fusion.2), kind=kOutput, calls=%fused_computation.46.clone.1 | convolution fusion | flops 543408128 | bytes 16843264 | tf_op jit(solution)/shard_map/while/body/eval_jaxpr/cnm,nk->ckm/dot_general | solution.py:39
  118.1 7.1 %fusion.109 = (bf16[128,128,128]{1,2,0:T(8,128)(2,1)S(1)}, bf16[128,128,128]{1,2,0:T(8,128)(2,1)S(1)}) fusion(f32[128,128,128]{2,1,0:T(8,128)S(1)} %fusion.108, f32[128,128]{0,1:T(8,128)S(1)} %get-tuple-element.171, f32[128,128]{0,1:T(8,128)S(1)} %get-tuple-element.172, f32[128,128,128]{1,2,0:T(8,128)} %copy.57, f32[128,128]{0,1:T(8,128)S(1)} %copy.58, ...), kind=kOutput, calls=%fused_computation.13.clone.1 | convolution fusion | flops 562282496 | bytes 25362944 | tf_op jit(solution)/shard_map/while/body/eval_jaxpr/cnm,nk->ckm/dot_general | solution.py:39
  127.5 1.0 add_bitcast_fusion.2
  128.6 2.1 %copy.59 = f32[128,33,128]{0,2,1:T(8,128)} copy(f32[128,33,128]{2,1,0:T(8,128)S(1)} %add_bitcast_fusion.2) | data formatting | bytes 4325376 | tf_op jit(solution)/shard_map/while/body/eval_jaxpr/add | solution.py:58
  131.3 3.0 %bitcast_multiply_fusion.6 = f32[1,128,4224]{1,2,0:T(8,128)S(1)} fusion(f32[128,33,128]{0,2,1:T(8,128)} %copy.59, f32[4224]{0:T(1024)S(1)} %select_divide_fusion.2), kind=kLoop, calls=%fused_computation.20.clone.1 | loop fusion | flops 540672 | bytes 4342272 | tf_op jit(solution)/shard_map/while/body/eval_jaxpr/mul | solution.py:58
  134.3 2.1 %copy.60 = f32[1,128,4224]{2,1,0:T(8,128)} copy(f32[1,128,4224]{1,2,0:T(8,128)S(1)} %bitcast_multiply_fusion.6) | data formatting | bytes 4325376 | tf_op jit(solution)/shard_map/while/body/jit(dynamic_update_index_in_dim)/dynamic_update_slice | solution.py:71
  136.4 3.1 %constant_dynamic-update-slice_fusion.2 = f32[2,128,4224]{2,1,0:T(8,128)} fusion(f32[2,128,4224]{2,1,0:T(8,128)} %get-tuple-element.181, f32[1,128,4224]{2,1,0:T(8,128)} %copy.60, s32[]{:T(128)} %get-tuple-element.180), kind=kLoop, calls=%fused_computation.72.clone.1 | loop fusion | bytes 4325888 | tf_op jit(solution)/shard_map/while/body/jit(dynamic_update_index_in_dim)/dynamic_update_slice | solution.py:71
  139.5 3.0 %convert_bitcast_fusion.2 = f32[16,8,128,128]{3,1,2,0:T(8,128)S(1)} fusion(bf16[2,128,16384]{2,1,0:T(8,128)(2,1)} %get-tuple-element.187, s32[]{:T(128)} %get-tuple-element.180), kind=kLoop, calls=%fused_computation.9.clone.1 | loop fusion | flops 2097152 | bytes 12582916 | tf_op jit(solution)/shard_map/while
  142.5 4.7 %copy.56 = f32[16,8,128,128]{3,2,1,0:T(8,128)} copy(f32[16,8,128,128]{3,1,2,0:T(8,128)S(1)} %convert_bitcast_fusion.2) | data formatting | bytes 16777216 | tf_op jit(solution)/shard_map/while
  147.2 9.0 %copy.57 = f32[128,128,128]{1,2,0:T(8,128)} copy(f32[128,128,128]{2,1,0:T(8,128)} %bitcast.95) | data formatting | bytes 16777216 | tf_op jit(solution)/shard_map/while/body/eval_jaxpr/convert_element_type | solution.py:45
  156.2 2.8 %convert_reduce_fusion.3 = f32[128]{0:T(128)S(1)} fusion(bf16[2,128,16384]{2,1,0:T(8,128)(2,1)} %get-tuple-element.187, s32[]{:T(128)} %get-tuple-element.180), kind=kLoop, calls=%fused_computation.8.clone.1 | loop fusion | flops 4194176 | bytes 4194820 | tf_op jit(solution)/shard_map/while/body/eval_jaxpr/reduce_sum | solution.py:46
  159.4 4.9 %fusion.108 = f32[128,128,128]{2,1,0:T(8,128)S(1)} fusion(f32[128,128,128]{1,2,0:T(8,128)} %copy.57, f32[128,128]{0,1:T(8,128)S(1)} %copy.58, f32[128]{0:T(128)S(1)} %broadcast_multiply_fusion.2), kind=kOutput, calls=%fused_computation.46.clone.1 | convolution fusion | flops 543408128 | bytes 16843264 | tf_op jit(solution)/shard_map/while/body/eval_jaxpr/cnm,nk->ckm/dot_general | solution.py:39
  164.6 7.1 %fusion.109 = (bf16[128,128,128]{1,2,0:T(8,128)(2,1)S(1)}, bf16[128,128,128]{1,2,0:T(8,128)(2,1)S(1)}) fusion(f32[128,128,128]{2,1,0:T(8,128)S(1)} %fusion.108, f32[128,128]{0,1:T(8,128)S(1)} %get-tuple-element.171, f32[128,128]{0,1:T(8,128)S(1)} %get-tuple-element.172, f32[128,128,128]{1,2,0:T(8,128)} %copy.57, f32[128,128]{0,1:T(8,128)S(1)} %copy.58, ...), kind=kOutput, calls=%fused_computation.13.clone.1 | convolution fusion | flops 562282496 | bytes 25362944 | tf_op jit(solution)/shard_map/while/body/eval_jaxpr/cnm,nk->ckm/dot_general | solution.py:39
  173.9 1.0 add_bitcast_fusion.2
  175.0 2.1 %copy.59 = f32[128,33,128]{0,2,1:T(8,128)} copy(f32[128,33,128]{2,1,0:T(8,128)S(1)} %add_bitcast_fusion.2) | data formatting | bytes 4325376 | tf_op jit(solution)/shard_map/while/body/eval_jaxpr/add | solution.py:58
  177.7 3.0 %bitcast_multiply_fusion.6 = f32[1,128,4224]{1,2,0:T(8,128)S(1)} fusion(f32[128,33,128]{0,2,1:T(8,128)} %copy.59, f32[4224]{0:T(1024)S(1)} %select_divide_fusion.2), kind=kLoop, calls=%fused_computation.20.clone.1 | loop fusion | flops 540672 | bytes 4342272 | tf_op jit(solution)/shard_map/while/body/eval_jaxpr/mul | solution.py:58
  180.7 2.1 %copy.60 = f32[1,128,4224]{2,1,0:T(8,128)} copy(f32[1,128,4224]{1,2,0:T(8,128)S(1)} %bitcast_multiply_fusion.6) | data formatting | bytes 4325376 | tf_op jit(solution)/shard_map/while/body/jit(dynamic_update_index_in_dim)/dynamic_update_slice | solution.py:71
  182.8 3.1 %constant_dynamic-update-slice_fusion.2 = f32[2,128,4224]{2,1,0:T(8,128)} fusion(f32[2,128,4224]{2,1,0:T(8,128)} %get-tuple-element.181, f32[1,128,4224]{2,1,0:T(8,128)} %copy.60, s32[]{:T(128)} %get-tuple-element.180), kind=kLoop, calls=%fused_computation.72.clone.1 | loop fusion | bytes 4325888 | tf_op jit(solution)/shard_map/while/body/jit(dynamic_update_index_in_dim)/dynamic_update_slice | solution.py:71
  185.9 2.8 %multiply_reduce_fusion = f32[8,4224]{1,0:T(8,128)S(1)} fusion(f32[8,32,4224]{2,1,0:T(8,128)} %bitcast.99, f32[8,32]{1,0:T(8,128)S(1)} %copy-done), kind=kLoop, calls=%fused_computation.93 | loop fusion | flops 2128896 | bytes 4461568 | tf_op jit(solution)/shard_map/reduce_sum | solution.py:91
  (30 shorter events, 10.5 us)
Async XLA Ops:
  17.1 55.9 %all-to-all-start.1 = ((bf16[16,8,16384]{2,1,0:T(8,128)(2,1)}), bf16[16,8,16384]{2,1,0:T(8,128)(2,1)}, u32[]{:S(2)}, u32[]{:S(2)}) async-start(bf16[16,8,16384]{2,1,0:T(8,128)(2,1)} %bitcast.100), calls=%async_computation.1 | async-start | bytes 8388608 | tf_op jit(solution)/shard_map/all_to_all | solution.py:79
  93.1 92.9 %copy-start = (f32[8,32]{1,0:T(8,128)S(1)}, f32[8,32]{1,0:T(8,128)}, u32[]{:S(2)}) copy-start(f32[8,32]{1,0:T(8,128)} %copy.37) | copy-start | bytes 3076
  185.9 2.8 %copy-start.1 = (f32[8]{0:T(128)S(1)}, f32[8]{0:T(128)}, u32[]{:S(2)}) copy-start(f32[8]{0:T(128)} %broadcast_maximum_fusion) | copy-start | bytes 100
where the time goes:
time: 191 us; the launch traced here: 189 us
  local copies, waits for them, and re-layouts  55.3 us (29%)
  waiting for transfers between devices  49 us (26%)
  other arithmetic  33.2 us (17%)
  matrix products  30.6 us (16%)
  blocking collectives  16.3 us (9%)
  starting transfers between devices  4.93 us (3%)
    all_to_all x1, waiting for transfers between devices, per_device(): lax.all_to_all(samples, 'chan', split_axis=0, concat_axis=1, tiled=True)  49 us
    dot_general x12, matrix products, contract(): return jnp.einsum(form, left, right, preferred_element_type=jnp.float32)  30.6 us
    convert_element_type x2, local copies, waits for them, and re-layouts, spectrum(): values = segment.astype(jnp.float32)  18 us
    all_to_all x1, blocking collectives, per_device(): lax.all_to_all(valid.astype(jnp.bfloat16), 'chan', split_axis=0, concat_a...  16.3 us
    dynamic_update_slice x4, local copies, waits for them, and re-layouts, block_power(): lax.map(one_block, segments.reshape(height // block_rows, block_rows, -1))  10.4 us
    while x2, local copies, waits for them, and re-layouts  9.36 us
    concatenate x1, other arithmetic, block_power(): segments = jnp.concatenate([leading, trailing], axis=1)  7.56 us
    mul x2, other arithmetic, spectrum(): (last_real * last_real + closing_quadrature_part * closing_quadrature_par...  6.09 us
  transfers between devices with their start and end apart: 1, of which 1 were waited for; matrix products, arithmetic and copies ran while one was open for 1% of the time, Pallas kernels for 0%

commit v1 on v0

--- a/solution.py
+++ b/solution.py
@@ -77,7 +77,15 @@
     half_len = RADIX * RADIX // 2
     moved_samples, moved_valid = (
         lax.all_to_all(samples, "chan", split_axis=0, concat_axis=1, tiled=True),
-        lax.all_to_all(valid.astype(jnp.bfloat16), "chan", split_axis=0, concat_axis=1, tiled=True),
+        jnp.concatenate(
+            lax.all_to_all(
+                jnp.stack(jnp.split(valid.astype(jnp.bfloat16), lax.axis_size("chan"), axis=0)),
+                "chan",
+                0,
+                0,
+            ),
+            axis=1,
+        ),
     )
     owned_rows = moved_samples.shape[0]
     record = jnp.concatenate(

time: 191 us -> 197 us (1.031)
  matrix products: 30.6 us -> 35.8 us
    dot_general x12, matrix products: 30.6 us -> 35.8 us  [contract(): return jnp.einsum(form, left, right, preferred_element_type=jnp.float32)]
    while x2 -> x10, local copies, waits for them, and re-layouts: 9.36 us -> 9.39 us
    while x2 -> x4, other arithmetic: 6.05 us -> 6.06 us
where the time goes in v1:
time: 197 us; the launch traced here: 196 us
  local copies, waits for them, and re-layouts  56.4 us (29%)
  waiting for transfers between devices  49 us (25%)
  matrix products  35.8 us (18%)
  other arithmetic  33.1 us (17%)
  blocking collectives  16.2 us (8%)
  starting transfers between devices  4.93 us (3%)
    all_to_all x1, waiting for transfers between devices, per_device(): lax.all_to_all(samples, 'chan', split_axis=0, concat_axis=1, tiled=True)  49 us
    dot_general x12, matrix products, contract(): return jnp.einsum(form, left, right, preferred_element_type=jnp.float32)  35.8 us
    convert_element_type x2, local copies, waits for them, and re-layouts, spectrum(): values = segment.astype(jnp.float32)  18 us
    all_to_all x1, blocking collectives, per_device(): lax.all_to_all(jnp.stack(jnp.split(valid.astype(jnp.bfloat16), lax.axis_s...  16.2 us
    dynamic_update_slice x4, local copies, waits for them, and re-layouts, block_power(): lax.map(one_block, segments.reshape(height // block_rows, block_rows, -1))  10.3 us
    while x10, local copies, waits for them, and re-layouts  9.39 us
    concatenate x1, other arithmetic, block_power(): segments = jnp.concatenate([leading, trailing], axis=1)  7.56 us
    mul x2, other arithmetic, spectrum(): (last_real * last_real + closing_quadrature_part * closing_quadrature_par...  6.09 us
  transfers between devices with their start and end apart: 1, of which 1 were waited for; matrix products, arithmetic and copies ran while one was open for 1% of the time, Pallas kernels for 0%

profile of v1, /device:TPU:1, one launch (start us, length us, event | category | flops | bytes accessed | tf_op | source)
XLA Modules:
  0.0 195.7 jit_solution(7876116745931648055)
XLA Ops:
  1.9 16.2 %all_to_all.24 = bf16[16,8,2]{1,2,0:T(2,128)(2,1)S(1)} all-to-all(bf16[16,8,2]{1,2,0:T(2,128)(2,1)S(1)} %constant_dynamic-update-slice_fusion.1), channel_id=1, replica_groups=mesh['tm'=8,'chan'=16] {'chan'}, dimensions={0} | all-to-all | bytes 1024 | tf_op jit(solution)/shard_map/all_to_all | solution.py:81
  18.1 4.9 %all-to-all-start.1 = ((bf16[16,8,16384]{2,1,0:T(8,128)(2,1)}), bf16[16,8,16384]{2,1,0:T(8,128)(2,1)}, u32[]{:S(2)}, u32[]{:S(2)}) async-start(bf16[16,8,16384]{2,1,0:T(8,128)(2,1)} %bitcast.132), calls=%async_computation.1 | async-start | bytes 8388608 | tf_op jit(solution)/shard_map/all_to_all | solution.py:79
  25.1 49.0 %all-to-all-done.1 = bf16[16,8,16384]{2,1,0:T(8,128)(2,1)} async-done(((bf16[16,8,16384]{2,1,0:T(8,128)(2,1)}), bf16[16,8,16384]{2,1,0:T(8,128)(2,1)}, u32[]{:S(2)}, u32[]{:S(2)}) %all-to-all-start.1) | async-done | bytes 4194336 | tf_op jit(solution)/shard_map/all_to_all | solution.py:79
  74.1 3.0 %concatenate.11 = bf16[8,270336]{1,0:T(8,128)(2,1)S(1)} pad(bf16[8,262144]{1,0:T(8,128)(2,1)} %bitcast.20, bf16[]{:T(256)} %constant.69.clone.1), padding=0_0x0_8192 | pad | bytes 8519682 | tf_op jit(solution)/shard_map/concatenate | solution.py:91
  77.1 0.9 fusion.80
  78.0 4.3 %copy.26 = bf16[8,32,8192]{2,1,0:T(8,128)(2,1)} copy(bf16[8,32,8192]{2,0,1:T(8,128)(2,1)S(1)} %get-tuple-element.141) | data formatting | bytes 8388608 | tf_op jit(solution)/shard_map/slice | solution.py:96
  82.3 4.2 %copy.25 = bf16[8,32,8192]{2,1,0:T(8,128)(2,1)} copy(bf16[8,32,8192]{2,0,1:T(8,128)(2,1)S(1)} %get-tuple-element.140) | data formatting | bytes 8388608 | tf_op jit(solution)/shard_map/slice | solution.py:95
  86.6 7.6 %pad_maximum_fusion = bf16[2,128,16384]{2,1,0:T(8,128)(2,1)} fusion(bf16[2,128,8192]{2,1,0:T(8,128)(2,1)} %bitcast.129, bf16[2,128,8192]{2,1,0:T(8,128)(2,1)} %bitcast.130), kind=kLoop, calls=%fused_computation.92 | loop fusion | flops 16777216 | bytes 16777216 | tf_op jit(solution)/shard_map/concatenate | solution.py:66
  94.1 98.0 %while.12 = (s32[]{:T(128)}, f32[2,128,4224]{2,1,0:T(8,128)}, bf16[2,128,16384]{2,1,0:T(8,128)(2,1)}, f32[]{:T(128)}, s32[]{:T(128)}) while((s32[]{:T(128)}, f32[2,128,4224]{2,1,0:T(8,128)}, bf16[2,128,16384]{2,1,0:T(8,128)(2,1)}, f32[]{:T(128)}, s32[]{:T(128)}) %tuple.31), condition=%wide.region_3.4_spmd.clone.clone, body=%wide.region_1.3_spmd.clone.clone.sunk | while | flops 1669451648 | bytes 167284368 | solution.py:71
  94.1 3.0 %convert_bitcast_fusion.2 = f32[16,8,128,128]{3,1,2,0:T(8,128)S(1)} fusion(bf16[2,128,16384]{2,1,0:T(8,128)(2,1)} %get-tuple-element.187, s32[]{:T(128)S(6)} %copy.51), kind=kLoop, calls=%fused_computation.9.clone.1 | loop fusion | flops 2097152 | bytes 12582916 | tf_op jit(solution)/shard_map/while
  97.2 4.7 %copy.43 = f32[16,8,128,128]{3,2,1,0:T(8,128)} copy(f32[16,8,128,128]{3,1,2,0:T(8,128)S(1)} %convert_bitcast_fusion.2) | data formatting | bytes 16777216 | tf_op jit(solution)/shard_map/while
  101.8 9.0 %copy.44 = f32[128,128,128]{1,2,0:T(8,128)} copy(f32[128,128,128]{2,1,0:T(8,128)} %bitcast.127) | data formatting | bytes 16777216 | tf_op jit(solution)/shard_map/while/body/eval_jaxpr/convert_element_type | solution.py:45
  111.2 2.8 %convert_reduce_fusion.3 = f32[128]{0:T(128)S(1)} fusion(bf16[2,128,16384]{2,1,0:T(8,128)(2,1)} %get-tuple-element.187, s32[]{:T(128)S(6)} %copy.51), kind=kLoop, calls=%fused_computation.8.clone.1 | loop fusion | flops 4194176 | bytes 4194820 | tf_op jit(solution)/shard_map/while/body/eval_jaxpr/reduce_sum | solution.py:46
  114.0 8.3 %fusion.108 = f32[128,128,128]{2,1,0:T(8,128)} fusion(f32[128,128,128]{1,2,0:T(8,128)} %copy.44, f32[128,128]{0,1:T(8,128)S(1)} %copy.45, f32[128]{0:T(128)S(1)} %broadcast_multiply_fusion.2), kind=kOutput, calls=%fused_computation.46.clone.1 | convolution fusion | flops 543408128 | bytes 16843264 | tf_op jit(solution)/shard_map/while/body/eval_jaxpr/cnm,nk->ckm/dot_general | solution.py:39
  122.6 6.4 %fusion.109 = (bf16[128,128,128]{1,2,0:T(8,128)(2,1)S(1)}, bf16[128,128,128]{1,2,0:T(8,128)(2,1)S(1)}) fusion(f32[128,128,128]{2,1,0:T(8,128)} %fusion.108, f32[128,128]{0,1:T(8,128)S(1)} %get-tuple-element.171, f32[128,128]{0,1:T(8,128)S(1)} %get-tuple-element.172, f32[128,128,128]{1,2,0:T(8,128)S(1)} %bitcast.126, f32[128,128]{0,1:T(8,128)S(1)} %copy.45, ...), kind=kOutput, calls=%fused_computation.13.clone.1 | convolution fusion | flops 562282496 | bytes 25362944 | tf_op jit(solution)/shard_map/while/body/eval_jaxpr/cnm,nk->ckm/dot_general | solution.py:39
  131.2 1.0 add_bitcast_fusion.2
  132.3 2.1 %copy.46 = f32[128,33,128]{0,2,1:T(8,128)} copy(f32[128,33,128]{2,1,0:T(8,128)S(1)} %add_bitcast_fusion.2) | data formatting | bytes 4325376 | tf_op jit(solution)/shard_map/while/body/eval_jaxpr/add | solution.py:58
  134.9 3.0 %bitcast_multiply_fusion.6 = f32[1,128,4224]{1,2,0:T(8,128)S(1)} fusion(f32[128,33,128]{0,2,1:T(8,128)} %copy.46, f32[4224]{0:T(1024)S(1)} %select_divide_fusion.2), kind=kLoop, calls=%fused_computation.20.clone.1 | loop fusion | flops 540672 | bytes 4342272 | tf_op jit(solution)/shard_map/while/body/eval_jaxpr/mul | solution.py:58
  138.0 2.1 %copy.47 = f32[1,128,4224]{2,1,0:T(8,128)} copy(f32[1,128,4224]{1,2,0:T(8,128)S(1)} %bitcast_multiply_fusion.6) | data formatting | bytes 4325376 | tf_op jit(solution)/shard_map/while/body/jit(dynamic_update_index_in_dim)/dynamic_update_slice | solution.py:71
  140.0 3.1 %constant_dynamic-update-slice_fusion.18 = f32[2,128,4224]{2,1,0:T(8,128)} fusion(f32[2,128,4224]{2,1,0:T(8,128)} %get-tuple-element.181, f32[1,128,4224]{2,1,0:T(8,128)} %copy.47, s32[]{:T(128)S(6)} %copy.51), kind=kLoop, calls=%fused_computation.72.clone.1 | loop fusion | bytes 4325380 | tf_op jit(solution)/shard_map/while/body/jit(dynamic_update_index_in_dim)/dynamic_update_slice | solution.py:71
  143.2 3.0 %convert_bitcast_fusion.2 = f32[16,8,128,128]{3,1,2,0:T(8,128)S(1)} fusion(bf16[2,128,16384]{2,1,0:T(8,128)(2,1)} %get-tuple-element.187, s32[]{:T(128)S(6)} %copy.51), kind=kLoop, calls=%fused_computation.9.clone.1 | loop fusion | flops 2097152 | bytes 12582916 | tf_op jit(solution)/shard_map/while
  146.2 4.7 %copy.43 = f32[16,8,128,128]{3,2,1,0:T(8,128)} copy(f32[16,8,128,128]{3,1,2,0:T(8,128)S(1)} %convert_bitcast_fusion.2) | data formatting | bytes 16777216 | tf_op jit(solution)/shard_map/while
  150.9 9.0 %copy.44 = f32[128,128,128]{1,2,0:T(8,128)} copy(f32[128,128,128]{2,1,0:T(8,128)} %bitcast.127) | data formatting | bytes 16777216 | tf_op jit(solution)/shard_map/while/body/eval_jaxpr/convert_element_type | solution.py:45
  160.2 2.8 %convert_reduce_fusion.3 = f32[128]{0:T(128)S(1)} fusion(bf16[2,128,16384]{2,1,0:T(8,128)(2,1)} %get-tuple-element.187, s32[]{:T(128)S(6)} %copy.51), kind=kLoop, calls=%fused_computation.8.clone.1 | loop fusion | flops 4194176 | bytes 4194820 | tf_op jit(solution)/shard_map/while/body/eval_jaxpr/reduce_sum | solution.py:46
  163.1 8.3 %fusion.108 = f32[128,128,128]{2,1,0:T(8,128)} fusion(f32[128,128,128]{1,2,0:T(8,128)} %copy.44, f32[128,128]{0,1:T(8,128)S(1)} %copy.45, f32[128]{0:T(128)S(1)} %broadcast_multiply_fusion.2), kind=kOutput, calls=%fused_computation.46.clone.1 | convolution fusion | flops 543408128 | bytes 16843264 | tf_op jit(solution)/shard_map/while/body/eval_jaxpr/cnm,nk->ckm/dot_general | solution.py:39
  171.7 6.4 %fusion.109 = (bf16[128,128,128]{1,2,0:T(8,128)(2,1)S(1)}, bf16[128,128,128]{1,2,0:T(8,128)(2,1)S(1)}) fusion(f32[128,128,128]{2,1,0:T(8,128)} %fusion.108, f32[128,128]{0,1:T(8,128)S(1)} %get-tuple-element.171, f32[128,128]{0,1:T(8,128)S(1)} %get-tuple-element.172, f32[128,128,128]{1,2,0:T(8,128)S(1)} %bitcast.126, f32[128,128]{0,1:T(8,128)S(1)} %copy.45, ...), kind=kOutput, calls=%fused_computation.13.clone.1 | convolution fusion | flops 562282496 | bytes 25362944 | tf_op jit(solution)/shard_map/while/body/eval_jaxpr/cnm,nk->ckm/dot_general | solution.py:39
  180.3 1.0 add_bitcast_fusion.2
  181.3 2.1 %copy.46 = f32[128,33,128]{0,2,1:T(8,128)} copy(f32[128,33,128]{2,1,0:T(8,128)S(1)} %add_bitcast_fusion.2) | data formatting | bytes 4325376 | tf_op jit(solution)/shard_map/while/body/eval_jaxpr/add | solution.py:58
  183.9 3.0 %bitcast_multiply_fusion.6 = f32[1,128,4224]{1,2,0:T(8,128)S(1)} fusion(f32[128,33,128]{0,2,1:T(8,128)} %copy.46, f32[4224]{0:T(1024)S(1)} %select_divide_fusion.2), kind=kLoop, calls=%fused_computation.20.clone.1 | loop fusion | flops 540672 | bytes 4342272 | tf_op jit(solution)/shard_map/while/body/eval_jaxpr/mul | solution.py:58
  187.0 2.1 %copy.47 = f32[1,128,4224]{2,1,0:T(8,128)} copy(f32[1,128,4224]{1,2,0:T(8,128)S(1)} %bitcast_multiply_fusion.6) | data formatting | bytes 4325376 | tf_op jit(solution)/shard_map/while/body/jit(dynamic_update_index_in_dim)/dynamic_update_slice | solution.py:71
  189.0 3.1 %constant_dynamic-update-slice_fusion.18 = f32[2,128,4224]{2,1,0:T(8,128)} fusion(f32[2,128,4224]{2,1,0:T(8,128)} %get-tuple-element.181, f32[1,128,4224]{2,1,0:T(8,128)} %copy.47, s32[]{:T(128)S(6)} %copy.51), kind=kLoop, calls=%fused_computation.72.clone.1 | loop fusion | bytes 4325380 | tf_op jit(solution)/shard_map/while/body/jit(dynamic_update_index_in_dim)/dynamic_update_slice | solution.py:71
  192.1 2.8 %multiply_reduce_fusion = f32[8,4224]{1,0:T(8,128)S(1)} fusion(f32[8,32,4224]{2,1,0:T(8,128)} %bitcast.131, f32[8,32]{1,0:T(8,128)S(1)} %copy-done), kind=kLoop, calls=%fused_computation.93 | loop fusion | flops 2128896 | bytes 4461568 | tf_op jit(solution)/shard_map/reduce_sum | solution.py:99
  (54 shorter events, 11.5 us)
Async XLA Ops:
  18.1 55.9 %all-to-all-start.1 = ((bf16[16,8,16384]{2,1,0:T(8,128)(2,1)}), bf16[16,8,16384]{2,1,0:T(8,128)(2,1)}, u32[]{:S(2)}, u32[]{:S(2)}) async-start(bf16[16,8,16384]{2,1,0:T(8,128)(2,1)} %bitcast.132), calls=%async_computation.1 | async-start | bytes 8388608 | tf_op jit(solution)/shard_map/all_to_all | solution.py:79
  94.1 98.0 %copy-start = (f32[8,32]{1,0:T(8,128)S(1)}, f32[8,32]{1,0:T(8,128)}, u32[]{:S(2)}) copy-start(f32[8,32]{1,0:T(8,128)} %copy.24) | copy-start | bytes 3076
  114.0 8.6 %slice-start = ((s8[8388608]{0:T(1024)(128)(4,1)}), s8[4194304]{0:T(1024)(128)(4,1)S(1)}, s32[]{:S(2)}) async-start(s8[8388608]{0:T(1024)(128)(4,1)} %bitcast.125), calls=%async_computation.2 | async-start | bytes 8388608 | tf_op jit(solution)/shard_map/while
  114.0 8.6 %slice-start.1 = ((s8[8388608]{0:T(1024)(128)(4,1)}), s8[4194304]{0:T(1024)(128)(4,1)S(1)}, s32[]{:S(2)}) async-start(s8[8388608]{0:T(1024)(128)(4,1)} %bitcast.125), calls=%async_computation.3 | async-start | bytes 8388608 | tf_op jit(solution)/shard_map/while
  163.0 8.6 %slice-start = ((s8[8388608]{0:T(1024)(128)(4,1)}), s8[4194304]{0:T(1024)(128)(4,1)S(1)}, s32[]{:S(2)}) async-start(s8[8388608]{0:T(1024)(128)(4,1)} %bitcast.125), calls=%async_computation.2 | async-start | bytes 8388608 | tf_op jit(solution)/shard_map/while
  163.0 8.6 %slice-start.1 = ((s8[8388608]{0:T(1024)(128)(4,1)}), s8[4194304]{0:T(1024)(128)(4,1)S(1)}, s32[]{:S(2)}) async-start(s8[8388608]{0:T(1024)(128)(4,1)} %bitcast.125), calls=%async_computation.3 | async-start | bytes 8388608 | tf_op jit(solution)/shard_map/while
  192.1 2.8 %copy-start.1 = (f32[8]{0:T(128)S(1)}, f32[8]{0:T(128)}, u32[]{:S(2)}) copy-start(f32[8]{0:T(128)} %broadcast_maximum_fusion) | copy-start | bytes 100
